TPU v7x, 32 devices: a whole 2x2x4 slice. The times are simulated.
32 devices in a mesh: mem: 4 (over z), gx: 4 (over y, core), gy: 2 (over x).
Axes of the slice: x: 2, y: 2, z: 4, core: 2. Of those that a mesh axis runs over, the one named last changes fastest.
Arguments:
- height: float32 [4, 4, 128, 256], P('mem', None, 'gx', 'gy'), may hold values from -4 to 4
- wind: float32 [4, 2, 4, 128, 256], P('mem', None, None, 'gx', 'gy'), may hold values from -0.8 to 0.8
- moisture: float32 [4, 4, 128, 256], P('mem', None, 'gx', 'gy'), may hold values from 0 to 2
- coeffs: float32 [4, 4, 4, 16384], P('mem', None, None, ('gx', 'gy')), may hold values from -6 to 6
- damping: float32 [16384], P(('gx', 'gy')), may hold values from 0.3 to 1
- vmix: float32 [4, 4], replicated, may hold values from -3 to 3
- basis: bfloat16 [16384, 384], P(('gx', 'gy')), may hold values from -0.046875 to 0.046875
- edge_source: int32 [768], replicated, may hold values from 0 to 383
- row_cell: int32 [128], replicated, may hold values from 0 to 15, never falling along the last dimension, each value on 1 to 16 neighbouring positions
- col_cell: int32 [256], replicated, may hold values from 0 to 31, never falling along the last dimension, each value on 1 to 16 neighbouring positions
- cond_rate: float32 [4], replicated, may hold values from 0.05 to 0.5
- saturation: float32 [4], replicated, may hold values from 0.5 to 1.5
- ancestry: int32 [4], replicated, may hold values from 0 to 3
Outputs:
- height_out: float32 [4, 4, 128, 256], P('mem', None, 'gx', 'gy')
- wind_out: float32 [4, 2, 4, 128, 256], P('mem', None, None, 'gx', 'gy')
- moisture_out: float32 [4, 4, 128, 256], P('mem', None, 'gx', 'gy')
- rainfall: float32 [4, 128, 256], P('mem', 'gx', 'gy')
- restricted: float32 [4, 4, 16, 32], P('mem')
- coeffs_out: float32 [4, 4, 4, 16384], P('mem', None, None, ('gx', 'gy'))
Inputs may be any that keep to these rules, and one draw needn't show every extreme that they name: row_cell never falls, and each of the 16 global rows holds 1 to 16 nest rows, one exactly 16. col_cell never falls, and each of the 32 global columns holds 1 to 16 nest columns, one exactly 16.
All inputs are finite; a program needn't handle non-finite values.
Results may differ from a plain program's by a relative error of at most 0.00035.
Values sent between devices are 32-bit elements; how exact they have to be, the bound alone decides.
A program may use at most 64 MiB of HBM per device.

v0:
```python
import jax
import jax.numpy as jnp
from jax import lax
from jax.sharding import PartitionSpec as P

RATIO = 8
ACOUSTIC = 2
acoustic_substep = 0.2
drift_step = 0.4


def extended(block, sides, width):
    for axis, dim in sides:
        count = lax.axis_size(axis)
        forward = [(i, i + 1) for i in range(count - 1)]
        backward = [(target, source) for source, target in forward]
        low = lax.ppermute(
            lax.slice_in_dim(block, block.shape[dim] - width, None, axis=dim), axis, forward
        )
        high = lax.ppermute(lax.slice_in_dim(block, 0, width, axis=dim), axis, backward)
        block = jnp.concatenate([low, block, high], axis=dim)
    return block


def side_values(rim, indices, rim_points, levels):
    table = (indices[None, :] == lax.iota(jnp.int32, rim_points)[:, None]).astype(jnp.float32)
    return jnp.dot(rim, table, precision=lax.Precision.HIGHEST).reshape(4, levels, indices.shape[0])


def frame(padded, sides, flags):
    western_edge, eastern_edge, southern_edge, northern_edge = sides
    at_west, at_east, at_south, at_north = flags
    size_x = padded.shape[2] - 2
    size_y = padded.shape[3] - 2
    current = padded[:, :, 0, 1 : 1 + size_y]
    padded = padded.at[:, :, 0, 1 : 1 + size_y].set(jnp.where(at_west, western_edge, current))
    current = padded[:, :, 1 + size_x, 1 : 1 + size_y]
    padded = padded.at[:, :, 1 + size_x, 1 : 1 + size_y].set(
        jnp.where(at_east, eastern_edge, current)
    )
    current = padded[:, :, 1 : 1 + size_x, 0]
    padded = padded.at[:, :, 1 : 1 + size_x, 0].set(jnp.where(at_south, southern_edge, current))
    current = padded[:, :, 1 : 1 + size_x, 1 + size_y]
    padded = padded.at[:, :, 1 : 1 + size_x, 1 + size_y].set(
        jnp.where(at_north, northern_edge, current)
    )
    return padded


def pick_sides(sides, first, last):
    return tuple((side[first:last] for side in sides))


def body(
    height,
    wind,
    moisture,
    coeffs,
    damping,
    vmix,
    basis,
    edge_source,
    row_cell,
    col_cell,
    cond_rate,
    saturation,
    ancestry,
):
    levels = height.shape[1]
    size_x = height.shape[2]
    size_y = height.shape[3]
    full_x = row_cell.shape[0]
    full_y = col_cell.shape[0]
    rim_points = basis.shape[1]
    row_index = lax.axis_index("gx")
    col_index = lax.axis_index("gy")
    row_start = row_index * size_x
    col_start = col_index * size_y
    coeff_new = jnp.einsum("lj,mfjk->mflk", vmix, coeffs, precision=lax.Precision.HIGHEST) * damping
    coeff_low = coeff_new.astype(jnp.bfloat16).reshape(4 * levels, -1)
    rim_part = jnp.dot(coeff_low, basis, preferred_element_type=jnp.float32)
    rim = lax.psum(rim_part, ("gx", "gy"))
    western_edge = side_values(
        rim, lax.dynamic_slice_in_dim(edge_source, col_start, size_y), rim_points, levels
    )
    eastern_edge = side_values(
        rim, lax.dynamic_slice_in_dim(edge_source, full_y + col_start, size_y), rim_points, levels
    )
    southern_edge = side_values(
        rim,
        lax.dynamic_slice_in_dim(edge_source, 2 * full_y + row_start, size_x),
        rim_points,
        levels,
    )
    northern_edge = side_values(
        rim,
        lax.dynamic_slice_in_dim(edge_source, 2 * full_y + full_x + row_start, size_x),
        rim_points,
        levels,
    )
    sides = (western_edge, eastern_edge, southern_edge, northern_edge)
    flags = (
        row_index == 0,
        row_index == lax.axis_size("gx") - 1,
        col_index == 0,
        col_index == lax.axis_size("gy") - 1,
    )
    h_field = height[0]
    u_field = wind[0, 0]
    v_field = wind[0, 1]
    q_field = moisture[0]
    for substep in range(ACOUSTIC):
        h_pad = extended(h_field[None], (("gx", 2), ("gy", 3)), 1)
        h_pad = frame(h_pad, pick_sides(sides, 0, 1), flags)[0]
        u_field = u_field - acoustic_substep * (h_pad[:, 2:, 1:-1] - h_pad[:, :-2, 1:-1])
        v_field = v_field - acoustic_substep * (h_pad[:, 1:-1, 2:] - h_pad[:, 1:-1, :-2])
        wind_pad = extended(jnp.stack([u_field, v_field]), (("gx", 2), ("gy", 3)), 1)
        wind_pad = frame(wind_pad, pick_sides(sides, 1, 3), flags)
        u_pad = wind_pad[0]
        v_pad = wind_pad[1]
        h_field = h_field - acoustic_substep * (
            u_pad[:, 2:, 1:-1] - u_pad[:, :-2, 1:-1] + (v_pad[:, 1:-1, 2:] - v_pad[:, 1:-1, :-2])
        )
    q_pad = extended(q_field[None], (("gx", 2), ("gy", 3)), 1)
    q_pad = frame(q_pad, pick_sides(sides, 3, 4), flags)[0]
    flux = (
        jnp.maximum(u_field, 0.0) * (q_field - q_pad[:, :-2, 1:-1])
        + jnp.minimum(u_field, 0.0) * (q_pad[:, 2:, 1:-1] - q_field)
        + (
            jnp.maximum(v_field, 0.0) * (q_field - q_pad[:, 1:-1, :-2])
            + jnp.minimum(v_field, 0.0) * (q_pad[:, 1:-1, 2:] - q_field)
        )
    )
    q_field = q_field - drift_step * flux
    excess = jnp.maximum(q_field - saturation[:, None, None], 0.0)
    fallen = cond_rate[:, None, None] * excess
    q_field = q_field - fallen
    rain = jnp.sum(fallen, axis=0)
    coarse_rows = full_x // RATIO
    coarse_cols = full_y // RATIO
    row_table = (row_cell[None, :] == lax.iota(jnp.int32, coarse_rows)[:, None]).astype(jnp.float32)
    col_table = (col_cell[None, :] == lax.iota(jnp.int32, coarse_cols)[:, None]).astype(jnp.float32)
    row_count = jnp.sum(row_table, axis=1)
    col_count = jnp.sum(col_table, axis=1)
    local_rows = lax.dynamic_slice_in_dim(row_table, row_start, size_x, 1)
    local_cols = lax.dynamic_slice_in_dim(col_table, col_start, size_y, 1)
    partial_value = jnp.einsum("ax,lxy->lay", local_rows, q_field, precision=lax.Precision.HIGHEST)
    partial_value = jnp.einsum(
        "lay,by->lab", partial_value, local_cols, precision=lax.Precision.HIGHEST
    )
    sums = lax.psum(partial_value, "gy")
    sums = lax.psum(sums, "gx")
    coarse = sums / (row_count[:, None] * col_count[None, :])
    states = (
        h_field[None],
        jnp.stack([u_field, v_field])[None],
        q_field[None],
        rain[None],
        coarse[None],
        coeff_new,
    )
    member_here = lax.axis_index("mem")
    everyone = (
        lax.all_gather(states[0], "mem", axis=0, tiled=True),
        lax.all_gather(states[1], "mem", axis=0, tiled=True),
        lax.all_gather(states[2], "mem", axis=0, tiled=True),
        lax.all_gather(states[3], "mem", axis=0, tiled=True),
        lax.all_gather(states[4], "mem", axis=0, tiled=True),
        lax.all_gather(states[5], "mem", axis=0, tiled=True),
    )
    source = ancestry[member_here]
    cloned = tuple(
        (lax.dynamic_index_in_dim(whole, source, 0, keepdims=True) for whole in everyone)
    )
    return (cloned[0], cloned[1], cloned[2], cloned[3], cloned[4], cloned[5])


def solution(mesh):
    in_specs = (
        P("mem", None, "gx", "gy"),
        P("mem", None, None, "gx", "gy"),
        P("mem", None, "gx", "gy"),
        P("mem", None, None, ("gx", "gy")),
        P(("gx", "gy")),
        P(),
        P(("gx", "gy"), None),
        P(),
        P(),
        P(),
        P(),
        P(),
        P(),
    )
    out_specs = (
        P("mem", None, "gx", "gy"),
        P("mem", None, None, "gx", "gy"),
        P("mem", None, "gx", "gy"),
        P("mem", "gx", "gy"),
        P("mem", None, None, None),
        P("mem", None, None, ("gx", "gy")),
    )
    return jax.shard_map(body, mesh=mesh, in_specs=in_specs, out_specs=out_specs, check_vma=False)
```

profile of v0, /device:TPU:10, one launch (start us, length us, event | category | flops | bytes accessed | tf_op | source)
XLA Modules:
  0.0 245.4 jit_solution(11485259475965265100)
XLA Ops:
  5.3 4.3 %collective-permute-start.16 = (f32[1,4,1,128]{3,1,2,0:T(4,128)S(1)}, f32[1,4,1,128]{3,1,2,0:T(4,128)S(1)}, u32[]{:S(2)}, u32[]{:S(2)}) collective-permute-start(f32[1,4,1,128]{3,1,2,0:T(4,128)S(1)} %copy.119), channel_id=1, source_target_pairs={{0,2},{2,4},{4,6},{1,3},{3,5},{5,7},{8,10},{10,12},{12,14},{9,11},... | collective-permute-start | bytes 6152 | tf_op jit(solution)/shard_map/ppermute | solution.py:17
  18.1 25.0 %psum.21 = f32[16,384]{1,0:T(8,128)S(1)} all-reduce(f32[16,384]{1,0:T(8,128)S(1)} %fusion.78), channel_id=1, replica_groups=mesh['mem'=4,'gx'=4,'gy'=2] {'gx','gy'}, use_global_device_ids=true, to_apply=%region_0.0 | all-reduce | flops 6144 | bytes 49152 | tf_op jit(solution)/shard_map/psum | solution.py:82
  44.0 16.5 %all_gather.23 = f32[4,4,4,2048]{3,2,1,0:T(4,128)S(1)} all-gather(f32[1,4,4,2048]{3,2,1,0:T(4,128)S(1)} %get-tuple-element.293), channel_id=1, replica_groups=mesh['mem'=4,'gx'=4,'gy'=2] {'mem'}, dimensions={0}, use_global_device_ids=true | all-gather | bytes 655360 | tf_op jit(solution)/shard_map/all_gather | solution.py:169
  63.0 3.3 %collective-permute-start.3 = (f32[1,4,34,1]{3,1,2,0:T(4,128)S(1)}, f32[1,4,34,1]{3,1,2,0:T(4,128)S(1)}, u32[]{:S(2)}, u32[]{:S(2)}) collective-permute-start(f32[1,4,34,1]{3,1,2,0:T(4,128)S(1)} %get-tuple-element.271), channel_id=1, source_target_pairs={{1,0},{3,2},{5,4},{7,6},{9,8},{11,10},{13,12},{15,14},{17,16},{19,... | collective-permute-start | bytes 1640 | tf_op jit(solution)/shard_map/ppermute | solution.py:20
  68.2 4.3 %collective-permute-done.2 = f32[1,4,34,1]{3,1,2,0:T(4,128)S(1)} collective-permute-done((f32[1,4,34,1]{3,1,2,0:T(4,128)S(1)}, f32[1,4,34,1]{3,1,2,0:T(4,128)S(1)}, u32[]{:S(2)}, u32[]{:S(2)}) %collective-permute-start.2) | collective-permute-done | bytes 576 | tf_op jit(solution)/shard_map/ppermute | solution.py:17
  75.2 2.4 scatter.71
  79.1 3.0 %collective-permute-start.4 = (f32[2,4,1,128]{3,1,2,0:T(4,128)S(1)}, f32[2,4,1,128]{3,1,2,0:T(4,128)S(1)}, u32[]{:S(2)}, u32[]{:S(2)}) collective-permute-start(f32[2,4,1,128]{3,1,2,0:T(4,128)S(1)} %get-tuple-element.262), channel_id=1, source_target_pairs={{0,2},{2,4},{4,6},{1,3},{3,5},{5,7},{8,10},{10,12},{12,14},{9,11},... | collective-permute-start | bytes 12296 | tf_op jit(solution)/shard_map/ppermute | solution.py:17
  85.4 4.6 %collective-permute-start.7 = (f32[2,4,34,1]{3,1,2,0:T(4,128)S(1)}, f32[2,4,34,1]{3,1,2,0:T(4,128)S(1)}, u32[]{:S(2)}, u32[]{:S(2)}) collective-permute-start(f32[2,4,34,1]{3,1,2,0:T(4,128)S(1)} %get-tuple-element.257), channel_id=1, source_target_pairs={{1,0},{3,2},{5,4},{7,6},{9,8},{11,10},{13,12},{15,14},{17,16},{19,... | collective-permute-start | bytes 3272 | tf_op jit(solution)/shard_map/ppermute | solution.py:20
  91.2 2.6 %collective-permute-done.7 = f32[2,4,34,1]{3,1,2,0:T(4,128)S(1)} collective-permute-done((f32[2,4,34,1]{3,1,2,0:T(4,128)S(1)}, f32[2,4,34,1]{3,1,2,0:T(4,128)S(1)}, u32[]{:S(2)}, u32[]{:S(2)}) %collective-permute-start.7) | collective-permute-done | bytes 1120 | tf_op jit(solution)/shard_map/ppermute | solution.py:20
  93.8 4.4 %collective-permute-done.6 = f32[2,4,34,1]{3,1,2,0:T(4,128)S(1)} collective-permute-done((f32[2,4,34,1]{3,1,2,0:T(4,128)S(1)}, f32[2,4,34,1]{3,1,2,0:T(4,128)S(1)}, u32[]{:S(2)}, u32[]{:S(2)}) %collective-permute-start.6) | collective-permute-done | bytes 1120 | tf_op jit(solution)/shard_map/ppermute | solution.py:17
  101.3 4.8 %scatter.79 = f32[2,4,34,130]{3,1,2,0:T(4,128)S(1)} dynamic-update-slice(f32[2,4,34,130]{3,1,2,0:T(4,128)S(1)} %scatter.76, f32[2,4,32,1]{3,1,2,0:T(4,128)S(1)} %slice_select_fusion.2, s32[]{:T(128)} %constant.509.clone.1, s32[]{:T(128)} %constant.509.clone.1, s32[]{:T(128)} %constant.516.clone.1, s32[]{:T(128)} %constant.522.clone.1) | dynamic-update-slice | bytes 2052 | tf_op jit(solution)/shard_map/scatter | solution.py:44
  116.0 3.4 %collective-permute-done.10 = f32[1,4,34,1]{3,1,2,0:T(4,128)S(1)} collective-permute-done((f32[1,4,34,1]{3,1,2,0:T(4,128)S(1)}, f32[1,4,34,1]{3,1,2,0:T(4,128)S(1)}, u32[]{:S(2)}, u32[]{:S(2)}) %collective-permute-start.10) | collective-permute-done | bytes 576 | tf_op jit(solution)/shard_map/ppermute | solution.py:17
  125.6 2.6 %scatter.85 = f32[4,34,130]{2,0,1:T(4,128)S(1)} dynamic-update-slice(f32[4,34,130]{2,0,1:T(4,128)S(1)} %bitcast.149, f32[4,32,1]{2,0,1:T(4,128)S(1)} %copy.88, s32[]{:T(128)} %constant.509.clone.1, s32[]{:T(128)} %constant.516.clone.1, s32[]{:T(128)} %constant.522.clone.1) | dynamic-update-slice | bytes 1028 | tf_op jit(solution)/shard_map/scatter | solution.py:44
  129.9 3.5 %collective-permute-start.12 = (f32[2,4,1,128]{3,1,2,0:T(4,128)S(1)}, f32[2,4,1,128]{3,1,2,0:T(4,128)S(1)}, u32[]{:S(2)}, u32[]{:S(2)}) collective-permute-start(f32[2,4,1,128]{3,1,2,0:T(4,128)S(1)} %get-tuple-element.260), channel_id=1, source_target_pairs={{0,2},{2,4},{4,6},{1,3},{3,5},{5,7},{8,10},{10,12},{12,14},{9,11},... | collective-permute-start | bytes 12296 | tf_op jit(solution)/shard_map/ppermute | solution.py:17
  133.4 16.1 %all-gather.1 = f32[8,4,32,128]{3,2,1,0:T(8,128)S(1)} all-gather(f32[2,4,32,128]{3,2,1,0:T(8,128)S(1)} %copy.92), channel_id=3, replica_groups=mesh['mem'=4,'gx'=4,'gy'=2] {'mem'}, dimensions={0}, use_global_device_ids=true | all-gather | bytes 655360 | tf_op jit(solution)/shard_map/all_gather | solution.py:165
  150.3 14.7 %all-gather.2 = f32[16,32,128]{2,1,0:T(8,128)S(1)} all-gather(f32[4,32,128]{2,1,0:T(8,128)S(1)} %copy.101), channel_id=4, replica_groups=mesh['mem'=4,'gx'=4,'gy'=2] {'mem'}, dimensions={0}, use_global_device_ids=true | all-gather | bytes 327680 | tf_op jit(solution)/shard_map/all_gather | solution.py:166
  165.7 13.2 %all-gather.3 = f32[128,128]{1,0:T(8,128)S(1)} all-gather(f32[32,128]{1,0:T(8,128)S(1)} %get-tuple-element.246), channel_id=5, replica_groups=mesh['mem'=4,'gx'=4,'gy'=2] {'mem'}, dimensions={0}, use_global_device_ids=true | all-gather | bytes 81920 | tf_op jit(solution)/shard_map/all_gather | solution.py:167
  179.2 7.0 %psum.22 = f32[4,16,32]{2,1,0:T(8,128)S(1)} all-reduce(f32[4,16,32]{2,1,0:T(8,128)S(1)} %fusion.36), channel_id=1, replica_groups=mesh['mem'=4,'gx'=4,'gy'=2] {'gy'}, use_global_device_ids=true, to_apply=%region_2.3 | all-reduce | flops 2048 | bytes 16384 | tf_op jit(solution)/shard_map/psum | solution.py:151
  186.2 10.3 %psum.23 = f32[4,16,32]{2,1,0:T(8,128)S(1)} all-reduce(f32[4,16,32]{2,1,0:T(8,128)S(1)} %psum.22), channel_id=1, replica_groups=mesh['mem'=4,'gx'=4,'gy'=2] {'gx'}, use_global_device_ids=true, to_apply=%region_3.4 | all-reduce | flops 2048 | bytes 16384 | tf_op jit(solution)/shard_map/psum | solution.py:152
  196.5 13.6 %all-gather.4 = f32[16,16,32]{2,1,0:T(8,128)S(1)} all-gather(f32[4,16,32]{2,1,0:T(8,128)S(1)} %broadcast_divide_fusion), channel_id=6, replica_groups=mesh['mem'=4,'gx'=4,'gy'=2] {'mem'}, dimensions={0}, use_global_device_ids=true | all-gather | bytes 40960 | tf_op jit(solution)/shard_map/all_gather | solution.py:168
  211.5 3.8 %collective-permute-start.15 = (f32[2,4,34,1]{3,1,2,0:T(4,128)S(1)}, f32[2,4,34,1]{3,1,2,0:T(4,128)S(1)}, u32[]{:S(2)}, u32[]{:S(2)}) collective-permute-start(f32[2,4,34,1]{3,1,2,0:T(4,128)S(1)} %get-tuple-element.255), channel_id=1, source_target_pairs={{1,0},{3,2},{5,4},{7,6},{9,8},{11,10},{13,12},{15,14},{17,16},{19,... | collective-permute-start | bytes 3272 | tf_op jit(solution)/shard_map/ppermute | solution.py:20
  217.9 4.4 %collective-permute-done.14 = f32[2,4,34,1]{3,1,2,0:T(4,128)S(1)} collective-permute-done((f32[2,4,34,1]{3,1,2,0:T(4,128)S(1)}, f32[2,4,34,1]{3,1,2,0:T(4,128)S(1)}, u32[]{:S(2)}, u32[]{:S(2)}) %collective-permute-start.14) | collective-permute-done | bytes 1120 | tf_op jit(solution)/shard_map/ppermute | solution.py:17
  225.3 4.8 %scatter.91 = f32[2,4,34,130]{3,1,2,0:T(4,128)S(1)} dynamic-update-slice(f32[2,4,34,130]{3,1,2,0:T(4,128)S(1)} %scatter.90, f32[2,4,32,1]{3,1,2,0:T(4,128)S(1)} %slice_select_fusion, s32[]{:T(128)} %constant.509.clone.1, s32[]{:T(128)} %constant.509.clone.1, s32[]{:T(128)} %constant.516.clone.1, s32[]{:T(128)} %constant.522.clone.1) | dynamic-update-slice | bytes 2052 | tf_op jit(solution)/shard_map/scatter | solution.py:44
  230.3 14.4 %all-gather = f32[16,32,128]{2,1,0:T(8,128)S(1)} all-gather(f32[4,32,128]{2,1,0:T(8,128)S(1)} %copy.91), channel_id=2, replica_groups=mesh['mem'=4,'gx'=4,'gy'=2] {'mem'}, dimensions={0}, use_global_device_ids=true | all-gather | bytes 327680 | tf_op jit(solution)/shard_map/all_gather | solution.py:164
  (165 shorter events, 55.0 us)
Async XLA Ops:
  0.6 42.4 %copy-start.6 = (s32[768]{0:T(1024)S(1)}, s32[768]{0:T(1024)}, u32[]{:S(2)}) copy-start(s32[768]{0:T(1024)} %param.60) | copy-start | bytes 9220
  0.7 43.3 %copy-start.3 = (f32[1,2,4,32,128]{4,3,2,1,0:T(8,128)S(1)}, f32[1,2,4,32,128]{4,3,2,1,0:T(8,128)}, u32[]{:S(2)}) copy-start(f32[1,2,4,32,128]{4,3,2,1,0:T(8,128)} %param.54) | copy-start | bytes 393220
  1.5 61.3 %collective-permute-start = (f32[1,4,1,128]{3,1,2,0:T(4,128)S(1)}, f32[1,4,1,128]{3,1,2,0:T(4,128)S(1)}, u32[]{:S(2)}, u32[]{:S(2)}) collective-permute-start(f32[1,4,1,128]{3,1,2,0:T(4,128)S(1)} %copy.117), channel_id=1, source_target_pairs={{0,2},{2,4},{4,6},{1,3},{3,5},{5,7},{8,10},{10,12},{12,14},{9,11},... | collective-permute-start | bytes 6152 | tf_op jit(solution)/shard_map/ppermute | solution.py:17
  3.3 59.6 %collective-permute-start.1 = (f32[1,4,1,128]{3,1,2,0:T(4,128)S(1)}, f32[1,4,1,128]{3,1,2,0:T(4,128)S(1)}, u32[]{:S(2)}, u32[]{:S(2)}) collective-permute-start(f32[1,4,1,128]{3,1,2,0:T(4,128)S(1)} %copy.118), channel_id=1, source_target_pairs={{2,0},{4,2},{6,4},{3,1},{5,3},{7,5},{10,8},{12,10},{14,12},{11,9},... | collective-permute-start | bytes 6152 | tf_op jit(solution)/shard_map/ppermute | solution.py:20
  5.3 62.2 %collective-permute-start.16 = (f32[1,4,1,128]{3,1,2,0:T(4,128)S(1)}, f32[1,4,1,128]{3,1,2,0:T(4,128)S(1)}, u32[]{:S(2)}, u32[]{:S(2)}) collective-permute-start(f32[1,4,1,128]{3,1,2,0:T(4,128)S(1)} %copy.119), channel_id=1, source_target_pairs={{0,2},{2,4},{4,6},{1,3},{3,5},{5,7},{8,10},{10,12},{12,14},{9,11},... | collective-permute-start | bytes 6152 | tf_op jit(solution)/shard_map/ppermute | solution.py:17
  9.7 58.0 %collective-permute-start.17 = (f32[1,4,1,128]{3,1,2,0:T(4,128)S(1)}, f32[1,4,1,128]{3,1,2,0:T(4,128)S(1)}, u32[]{:S(2)}, u32[]{:S(2)}) collective-permute-start(f32[1,4,1,128]{3,1,2,0:T(4,128)S(1)} %copy.120), channel_id=1, source_target_pairs={{2,0},{4,2},{6,4},{3,1},{5,3},{7,5},{10,8},{12,10},{14,12},{11,9},... | collective-permute-start | bytes 6152 | tf_op jit(solution)/shard_map/ppermute | solution.py:20
  17.8 45.0 %copy-start.2 = (f32[1,4,32,128]{3,2,1,0:T(8,128)S(1)}, f32[1,4,32,128]{3,2,1,0:T(8,128)}, u32[]{:S(2)}) copy-start(f32[1,4,32,128]{3,2,1,0:T(8,128)} %param.53) | copy-start | bytes 196612
  17.8 49.8 %copy-start.1 = (f32[1,4,32,128]{3,2,1,0:T(8,128)S(1)}, f32[1,4,32,128]{3,2,1,0:T(8,128)}, u32[]{:S(2)}) copy-start(f32[1,4,32,128]{3,2,1,0:T(8,128)} %param.55) | copy-start | bytes 196612
  63.0 5.2 %collective-permute-start.3 = (f32[1,4,34,1]{3,1,2,0:T(4,128)S(1)}, f32[1,4,34,1]{3,1,2,0:T(4,128)S(1)}, u32[]{:S(2)}, u32[]{:S(2)}) collective-permute-start(f32[1,4,34,1]{3,1,2,0:T(4,128)S(1)} %get-tuple-element.271), channel_id=1, source_target_pairs={{1,0},{3,2},{5,4},{7,6},{9,8},{11,10},{13,12},{15,14},{17,16},{19,... | collective-permute-start | bytes 1640 | tf_op jit(solution)/shard_map/ppermute | solution.py:20
  66.3 6.2 %collective-permute-start.2 = (f32[1,4,34,1]{3,1,2,0:T(4,128)S(1)}, f32[1,4,34,1]{3,1,2,0:T(4,128)S(1)}, u32[]{:S(2)}, u32[]{:S(2)}) collective-permute-start(f32[1,4,34,1]{3,1,2,0:T(4,128)S(1)} %get-tuple-element.270), channel_id=1, source_target_pairs={{0,1},{2,3},{4,5},{6,7},{8,9},{10,11},{12,13},{14,15},{16,17},{18,... | collective-permute-start | bytes 1640 | tf_op jit(solution)/shard_map/ppermute | solution.py:17
  77.8 7.3 %collective-permute-start.5 = (f32[2,4,1,128]{3,1,2,0:T(4,128)S(1)}, f32[2,4,1,128]{3,1,2,0:T(4,128)S(1)}, u32[]{:S(2)}, u32[]{:S(2)}) collective-permute-start(f32[2,4,1,128]{3,1,2,0:T(4,128)S(1)} %get-tuple-element.263), channel_id=1, source_target_pairs={{2,0},{4,2},{6,4},{3,1},{5,3},{7,5},{10,8},{12,10},{14,12},{11,9},... | collective-permute-start | bytes 12296 | tf_op jit(solution)/shard_map/ppermute | solution.py:20
  79.1 6.0 %collective-permute-start.4 = (f32[2,4,1,128]{3,1,2,0:T(4,128)S(1)}, f32[2,4,1,128]{3,1,2,0:T(4,128)S(1)}, u32[]{:S(2)}, u32[]{:S(2)}) collective-permute-start(f32[2,4,1,128]{3,1,2,0:T(4,128)S(1)} %get-tuple-element.262), channel_id=1, source_target_pairs={{0,2},{2,4},{4,6},{1,3},{3,5},{5,7},{8,10},{10,12},{12,14},{9,11},... | collective-permute-start | bytes 12296 | tf_op jit(solution)/shard_map/ppermute | solution.py:17
  82.3 27.3 %collective-permute-start.19 = (f32[1,4,34,1]{3,1,2,0:T(4,128)S(1)}, f32[1,4,34,1]{3,1,2,0:T(4,128)S(1)}, u32[]{:S(2)}, u32[]{:S(2)}) collective-permute-start(f32[1,4,34,1]{3,1,2,0:T(4,128)S(1)} %get-tuple-element.267), channel_id=1, source_target_pairs={{1,0},{3,2},{5,4},{7,6},{9,8},{11,10},{13,12},{15,14},{17,16},{19,... | collective-permute-start | bytes 1640 | tf_op jit(solution)/shard_map/ppermute | solution.py:20
  83.9 25.7 %collective-permute-start.18 = (f32[1,4,34,1]{3,1,2,0:T(4,128)S(1)}, f32[1,4,34,1]{3,1,2,0:T(4,128)S(1)}, u32[]{:S(2)}, u32[]{:S(2)}) collective-permute-start(f32[1,4,34,1]{3,1,2,0:T(4,128)S(1)} %get-tuple-element.266), channel_id=1, source_target_pairs={{0,1},{2,3},{4,5},{6,7},{8,9},{10,11},{12,13},{14,15},{16,17},{18,... | collective-permute-start | bytes 1640 | tf_op jit(solution)/shard_map/ppermute | solution.py:17
  85.4 8.4 %collective-permute-start.7 = (f32[2,4,34,1]{3,1,2,0:T(4,128)S(1)}, f32[2,4,34,1]{3,1,2,0:T(4,128)S(1)}, u32[]{:S(2)}, u32[]{:S(2)}) collective-permute-start(f32[2,4,34,1]{3,1,2,0:T(4,128)S(1)} %get-tuple-element.257), channel_id=1, source_target_pairs={{1,0},{3,2},{5,4},{7,6},{9,8},{11,10},{13,12},{15,14},{17,16},{19,... | collective-permute-start | bytes 3272 | tf_op jit(solution)/shard_map/ppermute | solution.py:20
  89.9 8.3 %collective-permute-start.6 = (f32[2,4,34,1]{3,1,2,0:T(4,128)S(1)}, f32[2,4,34,1]{3,1,2,0:T(4,128)S(1)}, u32[]{:S(2)}, u32[]{:S(2)}) collective-permute-start(f32[2,4,34,1]{3,1,2,0:T(4,128)S(1)} %get-tuple-element.256), channel_id=1, source_target_pairs={{0,1},{2,3},{4,5},{6,7},{8,9},{10,11},{12,13},{14,15},{16,17},{18,... | collective-permute-start | bytes 3272 | tf_op jit(solution)/shard_map/ppermute | solution.py:17
  106.3 3.4 %collective-permute-start.8 = (f32[1,4,1,128]{3,1,2,0:T(4,128)S(1)}, f32[1,4,1,128]{3,1,2,0:T(4,128)S(1)}, u32[]{:S(2)}, u32[]{:S(2)}) collective-permute-start(f32[1,4,1,128]{3,1,2,0:T(4,128)S(1)} %get-tuple-element.274), channel_id=1, source_target_pairs={{0,2},{2,4},{4,6},{1,3},{3,5},{5,7},{8,10},{10,12},{12,14},{9,11},... | collective-permute-start | bytes 6152 | tf_op jit(solution)/shard_map/ppermute | solution.py:17
  108.2 3.4 %collective-permute-start.9 = (f32[1,4,1,128]{3,1,2,0:T(4,128)S(1)}, f32[1,4,1,128]{3,1,2,0:T(4,128)S(1)}, u32[]{:S(2)}, u32[]{:S(2)}) collective-permute-start(f32[1,4,1,128]{3,1,2,0:T(4,128)S(1)} %get-tuple-element.275), channel_id=1, source_target_pairs={{2,0},{4,2},{6,4},{3,1},{5,3},{7,5},{10,8},{12,10},{14,12},{11,9},... | collective-permute-start | bytes 6152 | tf_op jit(solution)/shard_map/ppermute | solution.py:20
  111.7 4.3 %collective-permute-start.11 = (f32[1,4,34,1]{3,1,2,0:T(4,128)S(1)}, f32[1,4,34,1]{3,1,2,0:T(4,128)S(1)}, u32[]{:S(2)}, u32[]{:S(2)}) collective-permute-start(f32[1,4,34,1]{3,1,2,0:T(4,128)S(1)} %get-tuple-element.269), channel_id=1, source_target_pairs={{1,0},{3,2},{5,4},{7,6},{9,8},{11,10},{13,12},{15,14},{17,16},{19,... | collective-permute-start | bytes 1640 | tf_op jit(solution)/shard_map/ppermute | solution.py:20
  113.2 6.2 %collective-permute-start.10 = (f32[1,4,34,1]{3,1,2,0:T(4,128)S(1)}, f32[1,4,34,1]{3,1,2,0:T(4,128)S(1)}, u32[]{:S(2)}, u32[]{:S(2)}) collective-permute-start(f32[1,4,34,1]{3,1,2,0:T(4,128)S(1)} %get-tuple-element.268), channel_id=1, source_target_pairs={{0,1},{2,3},{4,5},{6,7},{8,9},{10,11},{12,13},{14,15},{16,17},{18,... | collective-permute-start | bytes 1640 | tf_op jit(solution)/shard_map/ppermute | solution.py:17
  128.6 82.7 %collective-permute-start.13 = (f32[2,4,1,128]{3,1,2,0:T(4,128)S(1)}, f32[2,4,1,128]{3,1,2,0:T(4,128)S(1)}, u32[]{:S(2)}, u32[]{:S(2)}) collective-permute-start(f32[2,4,1,128]{3,1,2,0:T(4,128)S(1)} %get-tuple-element.261), channel_id=1, source_target_pairs={{2,0},{4,2},{6,4},{3,1},{5,3},{7,5},{10,8},{12,10},{14,12},{11,9},... | collective-permute-start | bytes 12296 | tf_op jit(solution)/shard_map/ppermute | solution.py:20
  129.9 81.4 %collective-permute-start.12 = (f32[2,4,1,128]{3,1,2,0:T(4,128)S(1)}, f32[2,4,1,128]{3,1,2,0:T(4,128)S(1)}, u32[]{:S(2)}, u32[]{:S(2)}) collective-permute-start(f32[2,4,1,128]{3,1,2,0:T(4,128)S(1)} %get-tuple-element.260), channel_id=1, source_target_pairs={{0,2},{2,4},{4,6},{1,3},{3,5},{5,7},{8,10},{10,12},{12,14},{9,11},... | collective-permute-start | bytes 12296 | tf_op jit(solution)/shard_map/ppermute | solution.py:17
  211.5 6.4 %collective-permute-start.15 = (f32[2,4,34,1]{3,1,2,0:T(4,128)S(1)}, f32[2,4,34,1]{3,1,2,0:T(4,128)S(1)}, u32[]{:S(2)}, u32[]{:S(2)}) collective-permute-start(f32[2,4,34,1]{3,1,2,0:T(4,128)S(1)} %get-tuple-element.255), channel_id=1, source_target_pairs={{1,0},{3,2},{5,4},{7,6},{9,8},{11,10},{13,12},{15,14},{17,16},{19,... | collective-permute-start | bytes 3272 | tf_op jit(solution)/shard_map/ppermute | solution.py:20
  215.3 6.9 %collective-permute-start.14 = (f32[2,4,34,1]{3,1,2,0:T(4,128)S(1)}, f32[2,4,34,1]{3,1,2,0:T(4,128)S(1)}, u32[]{:S(2)}, u32[]{:S(2)}) collective-permute-start(f32[2,4,34,1]{3,1,2,0:T(4,128)S(1)} %get-tuple-element.254), channel_id=1, source_target_pairs={{0,1},{2,3},{4,5},{6,7},{8,9},{10,11},{12,13},{14,15},{16,17},{18,... | collective-permute-start | bytes 3272 | tf_op jit(solution)/shard_map/ppermute | solution.py:17
  (3 other events, 61.3 us)
where the time goes:
time: 246 us; the launch traced here: 245 us
  blocking collectives  131 us (53%)
  starting transfers between devices  42.1 us (17%)
  local copies, waits for them, and re-layouts  37.8 us (15%)
  waiting for transfers between devices  22.7 us (9%)
  other arithmetic  5.81 us (2%)
  between operations  3.52 us (1%)
  matrix products  2.68 us (1%)
    psum x1, blocking collectives, body(): rim = lax.psum(rim_part, ('gx', 'gy'))  25 us
    ppermute x10, starting transfers between devices, extended(): lax.ppermute(lax.slice_in_dim(block, 0, width, axis=dim), axis, backward)  21.2 us
    ppermute x10, starting transfers between devices, extended(): lax.ppermute(lax.slice_in_dim(block, block.shape[dim] - width, None, axis...  21 us
    scatter x5, local copies, waits for them, and re-layouts, frame(): padded.at[:, :, 1:1 + size_x, 1 + size_y]  16.9 us
    ppermute x10, waiting for transfers between devices, extended(): lax.ppermute(lax.slice_in_dim(block, block.shape[dim] - width, None, axis...  16.5 us
    all_gather x1, blocking collectives, body(): lax.all_gather(states[5], 'mem', axis=0, tiled=True)  16.5 us
    all_gather x1, blocking collectives, body(): lax.all_gather(states[1], 'mem', axis=0, tiled=True)  16.1 us
    all_gather x1, blocking collectives, body(): lax.all_gather(states[2], 'mem', axis=0, tiled=True)  14.7 us
  transfers between devices with their start and end apart: 20, of which 8 were waited for; matrix products, arithmetic and copies ran while one was open for 9% of the time, Pallas kernels for 0%

commit v1 on v0

--- a/solution.py
+++ b/solution.py
@@ -160,11 +160,34 @@
         coeff_new,
     )
     member_here = lax.axis_index("mem")
+
+    def hold_state(dim_no, group_axis, mine):
+        e_next, opened, work_now = (
+            lax.axis_size(group_axis),
+            lax.axis_index(group_axis),
+            mine.shape[dim_no],
+        )
+        b_next, mixed_arr = (mine, 1)
+        while mixed_arr < e_next:
+            b_next = jnp.concatenate(
+                [
+                    b_next,
+                    lax.ppermute(
+                        b_next,
+                        group_axis,
+                        tuple(((j, (j - mixed_arr) % e_next) for j in range(e_next))),
+                    ),
+                ],
+                axis=dim_no,
+            )
+            mixed_arr = 2 * mixed_arr
+        return jnp.roll(b_next, opened * work_now, axis=dim_no)
+
     everyone = (
         lax.all_gather(states[0], "mem", axis=0, tiled=True),
         lax.all_gather(states[1], "mem", axis=0, tiled=True),
         lax.all_gather(states[2], "mem", axis=0, tiled=True),
-        lax.all_gather(states[3], "mem", axis=0, tiled=True),
+        hold_state(0, "mem", states[3]),
         lax.all_gather(states[4], "mem", axis=0, tiled=True),
         lax.all_gather(states[5], "mem", axis=0, tiled=True),
     )

time: 246 us -> 242 us (0.984); the launches traced: 245 us -> 237 us
  blocking collectives: 131 us -> 117 us
  starting transfers between devices: 42.1 us -> 44.6 us
    all_gather x1 -> x0, blocking collectives: 13.2 us -> none  [body(): lax.all_gather(states[3], 'mem', axis=0, tiled=True)]
    ppermute x0 -> x2, starting transfers between devices: none -> 2.53 us  [hold_state(): lax.ppermute(b_next, group_axis, tuple(((j, (j - mixed_arr) % e_next) for...]
  transfers between devices with their start and end apart: 20 -> 22, of which waited for: 8 -> 9; matrix products, arithmetic and copies ran while one was open for 9% -> 13% of each run, Pallas kernels for 0% -> 0%
where the time goes in v1:
time: 242 us; the launch traced here: 237 us
  blocking collectives  117 us (48%)
  starting transfers between devices  44.6 us (18%)
  local copies, waits for them, and re-layouts  38.2 us (16%)
  waiting for transfers between devices  25 us (10%)
  other arithmetic  5.81 us (2%)
  between operations  3.55 us (1%)
  matrix products  2.68 us (1%)
    psum x1, blocking collectives, body(): rim = lax.psum(rim_part, ('gx', 'gy'))  25 us
    ppermute x10, starting transfers between devices, extended(): lax.ppermute(lax.slice_in_dim(block, 0, width, axis=dim), axis, backward)  21.1 us
    ppermute x10, starting transfers between devices, extended(): lax.ppermute(lax.slice_in_dim(block, block.shape[dim] - width, None, axis...  21 us
    scatter x5, local copies, waits for them, and re-layouts, frame(): padded.at[:, :, 1:1 + size_x, 1 + size_y]  16.9 us
    all_gather x1, blocking collectives, body(): lax.all_gather(states[5], 'mem', axis=0, tiled=True)  16.5 us
    ppermute x10, waiting for transfers between devices, extended(): lax.ppermute(lax.slice_in_dim(block, block.shape[dim] - width, None, axis...  16.4 us
    all_gather x1, blocking collectives, body(): lax.all_gather(states[1], 'mem', axis=0, tiled=True)  16.1 us
    all_gather x1, blocking collectives, body(): lax.all_gather(states[2], 'mem', axis=0, tiled=True)  14.7 us
  transfers between devices with their start and end apart: 22, of which 9 were waited for; matrix products, arithmetic and copies ran while one was open for 13% of the time, Pallas kernels for 0%

profile of v1, /device:TPU:10, one launch (start us, length us, event | category | flops | bytes accessed | tf_op | source)
XLA Modules:
  0.0 237.0 jit_solution(13891669978268073537)
XLA Ops:
  5.3 4.3 %collective-permute-start.16 = (f32[1,4,1,128]{3,1,2,0:T(4,128)S(1)}, f32[1,4,1,128]{3,1,2,0:T(4,128)S(1)}, u32[]{:S(2)}, u32[]{:S(2)}) collective-permute-start(f32[1,4,1,128]{3,1,2,0:T(4,128)S(1)} %copy.119), channel_id=1, source_target_pairs={{0,2},{2,4},{4,6},{1,3},{3,5},{5,7},{8,10},{10,12},{12,14},{9,11},... | collective-permute-start | bytes 6152 | tf_op jit(solution)/shard_map/ppermute | solution.py:17
  18.1 25.0 %psum.21 = f32[16,384]{1,0:T(8,128)S(1)} all-reduce(f32[16,384]{1,0:T(8,128)S(1)} %fusion.78), channel_id=1, replica_groups=mesh['mem'=4,'gx'=4,'gy'=2] {'gx','gy'}, use_global_device_ids=true, to_apply=%region_0.0 | all-reduce | flops 6144 | bytes 49152 | tf_op jit(solution)/shard_map/psum | solution.py:82
  44.0 16.5 %all_gather.19 = f32[4,4,4,2048]{3,2,1,0:T(4,128)S(1)} all-gather(f32[1,4,4,2048]{3,2,1,0:T(4,128)S(1)} %get-tuple-element.293), channel_id=1, replica_groups=mesh['mem'=4,'gx'=4,'gy'=2] {'mem'}, dimensions={0}, use_global_device_ids=true | all-gather | bytes 655360 | tf_op jit(solution)/shard_map/all_gather | solution.py:192
  63.0 3.3 %collective-permute-start.3 = (f32[1,4,34,1]{3,1,2,0:T(4,128)S(1)}, f32[1,4,34,1]{3,1,2,0:T(4,128)S(1)}, u32[]{:S(2)}, u32[]{:S(2)}) collective-permute-start(f32[1,4,34,1]{3,1,2,0:T(4,128)S(1)} %get-tuple-element.271), channel_id=1, source_target_pairs={{1,0},{3,2},{5,4},{7,6},{9,8},{11,10},{13,12},{15,14},{17,16},{19,... | collective-permute-start | bytes 1640 | tf_op jit(solution)/shard_map/ppermute | solution.py:20
  68.2 4.3 %collective-permute-done.2 = f32[1,4,34,1]{3,1,2,0:T(4,128)S(1)} collective-permute-done((f32[1,4,34,1]{3,1,2,0:T(4,128)S(1)}, f32[1,4,34,1]{3,1,2,0:T(4,128)S(1)}, u32[]{:S(2)}, u32[]{:S(2)}) %collective-permute-start.2) | collective-permute-done | bytes 576 | tf_op jit(solution)/shard_map/ppermute | solution.py:17
  75.3 2.4 %scatter.71 = f32[4,34,130]{2,0,1:T(4,128)S(1)} dynamic-update-slice(f32[4,34,130]{2,0,1:T(4,128)S(1)} %bitcast.152, f32[4,32,1]{2,0,1:T(4,128)S(1)} %copy.81, s32[]{:T(128)} %constant.540.clone.1, s32[]{:T(128)} %constant.547.clone.1, s32[]{:T(128)} %constant.553.clone.1) | dynamic-update-slice | bytes 1028 | tf_op jit(solution)/shard_map/scatter | solution.py:44
  79.2 3.0 %collective-permute-start.4 = (f32[2,4,1,128]{3,1,2,0:T(4,128)S(1)}, f32[2,4,1,128]{3,1,2,0:T(4,128)S(1)}, u32[]{:S(2)}, u32[]{:S(2)}) collective-permute-start(f32[2,4,1,128]{3,1,2,0:T(4,128)S(1)} %get-tuple-element.262), channel_id=1, source_target_pairs={{0,2},{2,4},{4,6},{1,3},{3,5},{5,7},{8,10},{10,12},{12,14},{9,11},... | collective-permute-start | bytes 12296 | tf_op jit(solution)/shard_map/ppermute | solution.py:17
  85.5 4.6 %collective-permute-start.7 = (f32[2,4,34,1]{3,1,2,0:T(4,128)S(1)}, f32[2,4,34,1]{3,1,2,0:T(4,128)S(1)}, u32[]{:S(2)}, u32[]{:S(2)}) collective-permute-start(f32[2,4,34,1]{3,1,2,0:T(4,128)S(1)} %get-tuple-element.257), channel_id=1, source_target_pairs={{1,0},{3,2},{5,4},{7,6},{9,8},{11,10},{13,12},{15,14},{17,16},{19,... | collective-permute-start | bytes 3272 | tf_op jit(solution)/shard_map/ppermute | solution.py:20
  91.3 2.6 %collective-permute-done.7 = f32[2,4,34,1]{3,1,2,0:T(4,128)S(1)} collective-permute-done((f32[2,4,34,1]{3,1,2,0:T(4,128)S(1)}, f32[2,4,34,1]{3,1,2,0:T(4,128)S(1)}, u32[]{:S(2)}, u32[]{:S(2)}) %collective-permute-start.7) | collective-permute-done | bytes 1120 | tf_op jit(solution)/shard_map/ppermute | solution.py:20
  93.9 4.4 %collective-permute-done.6 = f32[2,4,34,1]{3,1,2,0:T(4,128)S(1)} collective-permute-done((f32[2,4,34,1]{3,1,2,0:T(4,128)S(1)}, f32[2,4,34,1]{3,1,2,0:T(4,128)S(1)}, u32[]{:S(2)}, u32[]{:S(2)}) %collective-permute-start.6) | collective-permute-done | bytes 1120 | tf_op jit(solution)/shard_map/ppermute | solution.py:17
  101.5 4.8 %scatter.79 = f32[2,4,34,130]{3,1,2,0:T(4,128)S(1)} dynamic-update-slice(f32[2,4,34,130]{3,1,2,0:T(4,128)S(1)} %scatter.76, f32[2,4,32,1]{3,1,2,0:T(4,128)S(1)} %slice_select_fusion.2, s32[]{:T(128)} %constant.540.clone.1, s32[]{:T(128)} %constant.540.clone.1, s32[]{:T(128)} %constant.547.clone.1, s32[]{:T(128)} %constant.553.clone.1) | dynamic-update-slice | bytes 2052 | tf_op jit(solution)/shard_map/scatter | solution.py:44
  116.3 3.3 %collective-permute-done.10 = f32[1,4,34,1]{3,1,2,0:T(4,128)S(1)} collective-permute-done((f32[1,4,34,1]{3,1,2,0:T(4,128)S(1)}, f32[1,4,34,1]{3,1,2,0:T(4,128)S(1)}, u32[]{:S(2)}, u32[]{:S(2)}) %collective-permute-start.10) | collective-permute-done | bytes 576 | tf_op jit(solution)/shard_map/ppermute | solution.py:17
  125.9 2.6 %scatter.85 = f32[4,34,130]{2,0,1:T(4,128)S(1)} dynamic-update-slice(f32[4,34,130]{2,0,1:T(4,128)S(1)} %bitcast.151, f32[4,32,1]{2,0,1:T(4,128)S(1)} %copy.88, s32[]{:T(128)} %constant.540.clone.1, s32[]{:T(128)} %constant.547.clone.1, s32[]{:T(128)} %constant.553.clone.1) | dynamic-update-slice | bytes 1028 | tf_op jit(solution)/shard_map/scatter | solution.py:44
  130.1 3.5 %collective-permute-start.12 = (f32[2,4,1,128]{3,1,2,0:T(4,128)S(1)}, f32[2,4,1,128]{3,1,2,0:T(4,128)S(1)}, u32[]{:S(2)}, u32[]{:S(2)}) collective-permute-start(f32[2,4,1,128]{3,1,2,0:T(4,128)S(1)} %get-tuple-element.260), channel_id=1, source_target_pairs={{0,2},{2,4},{4,6},{1,3},{3,5},{5,7},{8,10},{10,12},{12,14},{9,11},... | collective-permute-start | bytes 12296 | tf_op jit(solution)/shard_map/ppermute | solution.py:17
  133.7 16.1 %all-gather.1 = f32[8,4,32,128]{3,2,1,0:T(8,128)S(1)} all-gather(f32[2,4,32,128]{3,2,1,0:T(8,128)S(1)} %copy.92), channel_id=3, replica_groups=mesh['mem'=4,'gx'=4,'gy'=2] {'mem'}, dimensions={0}, use_global_device_ids=true | all-gather | bytes 655360 | tf_op jit(solution)/shard_map/all_gather | solution.py:188
  150.5 14.7 %all-gather.2 = f32[16,32,128]{2,1,0:T(8,128)S(1)} all-gather(f32[4,32,128]{2,1,0:T(8,128)S(1)} %copy.101), channel_id=4, replica_groups=mesh['mem'=4,'gx'=4,'gy'=2] {'mem'}, dimensions={0}, use_global_device_ids=true | all-gather | bytes 327680 | tf_op jit(solution)/shard_map/all_gather | solution.py:189
  166.4 7.0 %psum.22 = f32[4,16,32]{2,1,0:T(8,128)S(1)} all-reduce(f32[4,16,32]{2,1,0:T(8,128)S(1)} %fusion.36), channel_id=1, replica_groups=mesh['mem'=4,'gx'=4,'gy'=2] {'gy'}, use_global_device_ids=true, to_apply=%region_2.3 | all-reduce | flops 2048 | bytes 16384 | tf_op jit(solution)/shard_map/psum | solution.py:151
  173.4 10.3 %psum.23 = f32[4,16,32]{2,1,0:T(8,128)S(1)} all-reduce(f32[4,16,32]{2,1,0:T(8,128)S(1)} %psum.22), channel_id=1, replica_groups=mesh['mem'=4,'gx'=4,'gy'=2] {'gx'}, use_global_device_ids=true, to_apply=%region_3.4 | all-reduce | flops 2048 | bytes 16384 | tf_op jit(solution)/shard_map/psum | solution.py:152
  183.7 13.4 %all-gather.3 = f32[16,16,32]{2,1,0:T(8,128)S(1)} all-gather(f32[4,16,32]{2,1,0:T(8,128)S(1)} %broadcast_divide_fusion), channel_id=5, replica_groups=mesh['mem'=4,'gx'=4,'gy'=2] {'mem'}, dimensions={0}, use_global_device_ids=true | all-gather | bytes 40960 | tf_op jit(solution)/shard_map/all_gather | solution.py:191
  197.9 3.7 %collective-permute-start.15 = (f32[2,4,34,1]{3,1,2,0:T(4,128)S(1)}, f32[2,4,34,1]{3,1,2,0:T(4,128)S(1)}, u32[]{:S(2)}, u32[]{:S(2)}) collective-permute-start(f32[2,4,34,1]{3,1,2,0:T(4,128)S(1)} %get-tuple-element.255), channel_id=1, source_target_pairs={{1,0},{3,2},{5,4},{7,6},{9,8},{11,10},{13,12},{15,14},{17,16},{19,... | collective-permute-start | bytes 3272 | tf_op jit(solution)/shard_map/ppermute | solution.py:20
  204.2 4.4 %collective-permute-done.14 = f32[2,4,34,1]{3,1,2,0:T(4,128)S(1)} collective-permute-done((f32[2,4,34,1]{3,1,2,0:T(4,128)S(1)}, f32[2,4,34,1]{3,1,2,0:T(4,128)S(1)}, u32[]{:S(2)}, u32[]{:S(2)}) %collective-permute-start.14) | collective-permute-done | bytes 1120 | tf_op jit(solution)/shard_map/ppermute | solution.py:17
  211.7 4.8 %scatter.91 = f32[2,4,34,130]{3,1,2,0:T(4,128)S(1)} dynamic-update-slice(f32[2,4,34,130]{3,1,2,0:T(4,128)S(1)} %scatter.90, f32[2,4,32,1]{3,1,2,0:T(4,128)S(1)} %slice_select_fusion, s32[]{:T(128)} %constant.540.clone.1, s32[]{:T(128)} %constant.540.clone.1, s32[]{:T(128)} %constant.547.clone.1, s32[]{:T(128)} %constant.553.clone.1) | dynamic-update-slice | bytes 2052 | tf_op jit(solution)/shard_map/scatter | solution.py:44
  216.7 14.2 %all-gather = f32[16,32,128]{2,1,0:T(8,128)S(1)} all-gather(f32[4,32,128]{2,1,0:T(8,128)S(1)} %copy.91), channel_id=2, replica_groups=mesh['mem'=4,'gx'=4,'gy'=2] {'mem'}, dimensions={0}, use_global_device_ids=true | all-gather | bytes 327680 | tf_op jit(solution)/shard_map/all_gather | solution.py:187
  231.6 2.5 %collective-permute-start.21 = (f32[2,32,128]{2,1,0:T(8,128)S(1)}, f32[2,32,128]{2,1,0:T(8,128)S(1)}, u32[]{:S(2)}, u32[]{:S(2)}) collective-permute-start(f32[2,32,128]{2,1,0:T(8,128)S(1)} %pad_maximum_fusion.9), channel_id=1, source_target_pairs={{0,16},{8,24},{16,0},{24,8},{1,17},{9,25},{17,1},{25,9},{2,18},{10... | collective-permute-start | bytes 98312 | tf_op jit(solution)/shard_map/ppermute | solution.py:175
  (175 shorter events, 57.9 us)
Async XLA Ops:
  1.5 61.3 %collective-permute-start = (f32[1,4,1,128]{3,1,2,0:T(4,128)S(1)}, f32[1,4,1,128]{3,1,2,0:T(4,128)S(1)}, u32[]{:S(2)}, u32[]{:S(2)}) collective-permute-start(f32[1,4,1,128]{3,1,2,0:T(4,128)S(1)} %copy.117), channel_id=1, source_target_pairs={{0,2},{2,4},{4,6},{1,3},{3,5},{5,7},{8,10},{10,12},{12,14},{9,11},... | collective-permute-start | bytes 6152 | tf_op jit(solution)/shard_map/ppermute | solution.py:17
  3.3 59.6 %collective-permute-start.1 = (f32[1,4,1,128]{3,1,2,0:T(4,128)S(1)}, f32[1,4,1,128]{3,1,2,0:T(4,128)S(1)}, u32[]{:S(2)}, u32[]{:S(2)}) collective-permute-start(f32[1,4,1,128]{3,1,2,0:T(4,128)S(1)} %copy.118), channel_id=1, source_target_pairs={{2,0},{4,2},{6,4},{3,1},{5,3},{7,5},{10,8},{12,10},{14,12},{11,9},... | collective-permute-start | bytes 6152 | tf_op jit(solution)/shard_map/ppermute | solution.py:20
  5.3 62.3 %collective-permute-start.16 = (f32[1,4,1,128]{3,1,2,0:T(4,128)S(1)}, f32[1,4,1,128]{3,1,2,0:T(4,128)S(1)}, u32[]{:S(2)}, u32[]{:S(2)}) collective-permute-start(f32[1,4,1,128]{3,1,2,0:T(4,128)S(1)} %copy.119), channel_id=1, source_target_pairs={{0,2},{2,4},{4,6},{1,3},{3,5},{5,7},{8,10},{10,12},{12,14},{9,11},... | collective-permute-start | bytes 6152 | tf_op jit(solution)/shard_map/ppermute | solution.py:17
  9.7 58.0 %collective-permute-start.17 = (f32[1,4,1,128]{3,1,2,0:T(4,128)S(1)}, f32[1,4,1,128]{3,1,2,0:T(4,128)S(1)}, u32[]{:S(2)}, u32[]{:S(2)}) collective-permute-start(f32[1,4,1,128]{3,1,2,0:T(4,128)S(1)} %copy.120), channel_id=1, source_target_pairs={{2,0},{4,2},{6,4},{3,1},{5,3},{7,5},{10,8},{12,10},{14,12},{11,9},... | collective-permute-start | bytes 6152 | tf_op jit(solution)/shard_map/ppermute | solution.py:20
  17.8 45.1 %copy-start.2 = (f32[1,4,32,128]{3,2,1,0:T(8,128)S(1)}, f32[1,4,32,128]{3,2,1,0:T(8,128)}, u32[]{:S(2)}) copy-start(f32[1,4,32,128]{3,2,1,0:T(8,128)} %param.53) | copy-start | bytes 196612
  17.8 49.8 %copy-start.1 = (f32[1,4,32,128]{3,2,1,0:T(8,128)S(1)}, f32[1,4,32,128]{3,2,1,0:T(8,128)}, u32[]{:S(2)}) copy-start(f32[1,4,32,128]{3,2,1,0:T(8,128)} %param.55) | copy-start | bytes 196612
  63.0 5.2 %collective-permute-start.3 = (f32[1,4,34,1]{3,1,2,0:T(4,128)S(1)}, f32[1,4,34,1]{3,1,2,0:T(4,128)S(1)}, u32[]{:S(2)}, u32[]{:S(2)}) collective-permute-start(f32[1,4,34,1]{3,1,2,0:T(4,128)S(1)} %get-tuple-element.271), channel_id=1, source_target_pairs={{1,0},{3,2},{5,4},{7,6},{9,8},{11,10},{13,12},{15,14},{17,16},{19,... | collective-permute-start | bytes 1640 | tf_op jit(solution)/shard_map/ppermute | solution.py:20
  66.3 6.2 %collective-permute-start.2 = (f32[1,4,34,1]{3,1,2,0:T(4,128)S(1)}, f32[1,4,34,1]{3,1,2,0:T(4,128)S(1)}, u32[]{:S(2)}, u32[]{:S(2)}) collective-permute-start(f32[1,4,34,1]{3,1,2,0:T(4,128)S(1)} %get-tuple-element.270), channel_id=1, source_target_pairs={{0,1},{2,3},{4,5},{6,7},{8,9},{10,11},{12,13},{14,15},{16,17},{18,... | collective-permute-start | bytes 1640 | tf_op jit(solution)/shard_map/ppermute | solution.py:17
  77.9 7.3 %collective-permute-start.5 = (f32[2,4,1,128]{3,1,2,0:T(4,128)S(1)}, f32[2,4,1,128]{3,1,2,0:T(4,128)S(1)}, u32[]{:S(2)}, u32[]{:S(2)}) collective-permute-start(f32[2,4,1,128]{3,1,2,0:T(4,128)S(1)} %get-tuple-element.263), channel_id=1, source_target_pairs={{2,0},{4,2},{6,4},{3,1},{5,3},{7,5},{10,8},{12,10},{14,12},{11,9},... | collective-permute-start | bytes 12296 | tf_op jit(solution)/shard_map/ppermute | solution.py:20
  79.2 6.0 %collective-permute-start.4 = (f32[2,4,1,128]{3,1,2,0:T(4,128)S(1)}, f32[2,4,1,128]{3,1,2,0:T(4,128)S(1)}, u32[]{:S(2)}, u32[]{:S(2)}) collective-permute-start(f32[2,4,1,128]{3,1,2,0:T(4,128)S(1)} %get-tuple-element.262), channel_id=1, source_target_pairs={{0,2},{2,4},{4,6},{1,3},{3,5},{5,7},{8,10},{10,12},{12,14},{9,11},... | collective-permute-start | bytes 12296 | tf_op jit(solution)/shard_map/ppermute | solution.py:17
  82.4 27.3 %collective-permute-start.19 = (f32[1,4,34,1]{3,1,2,0:T(4,128)S(1)}, f32[1,4,34,1]{3,1,2,0:T(4,128)S(1)}, u32[]{:S(2)}, u32[]{:S(2)}) collective-permute-start(f32[1,4,34,1]{3,1,2,0:T(4,128)S(1)} %get-tuple-element.267), channel_id=1, source_target_pairs={{1,0},{3,2},{5,4},{7,6},{9,8},{11,10},{13,12},{15,14},{17,16},{19,... | collective-permute-start | bytes 1640 | tf_op jit(solution)/shard_map/ppermute | solution.py:20
  84.0 25.8 %collective-permute-start.18 = (f32[1,4,34,1]{3,1,2,0:T(4,128)S(1)}, f32[1,4,34,1]{3,1,2,0:T(4,128)S(1)}, u32[]{:S(2)}, u32[]{:S(2)}) collective-permute-start(f32[1,4,34,1]{3,1,2,0:T(4,128)S(1)} %get-tuple-element.266), channel_id=1, source_target_pairs={{0,1},{2,3},{4,5},{6,7},{8,9},{10,11},{12,13},{14,15},{16,17},{18,... | collective-permute-start | bytes 1640 | tf_op jit(solution)/shard_map/ppermute | solution.py:17
  85.5 8.4 %collective-permute-start.7 = (f32[2,4,34,1]{3,1,2,0:T(4,128)S(1)}, f32[2,4,34,1]{3,1,2,0:T(4,128)S(1)}, u32[]{:S(2)}, u32[]{:S(2)}) collective-permute-start(f32[2,4,34,1]{3,1,2,0:T(4,128)S(1)} %get-tuple-element.257), channel_id=1, source_target_pairs={{1,0},{3,2},{5,4},{7,6},{9,8},{11,10},{13,12},{15,14},{17,16},{19,... | collective-permute-start | bytes 3272 | tf_op jit(solution)/shard_map/ppermute | solution.py:20
  90.0 8.3 %collective-permute-start.6 = (f32[2,4,34,1]{3,1,2,0:T(4,128)S(1)}, f32[2,4,34,1]{3,1,2,0:T(4,128)S(1)}, u32[]{:S(2)}, u32[]{:S(2)}) collective-permute-start(f32[2,4,34,1]{3,1,2,0:T(4,128)S(1)} %get-tuple-element.256), channel_id=1, source_target_pairs={{0,1},{2,3},{4,5},{6,7},{8,9},{10,11},{12,13},{14,15},{16,17},{18,... | collective-permute-start | bytes 3272 | tf_op jit(solution)/shard_map/ppermute | solution.py:17
  106.5 3.4 %collective-permute-start.8 = (f32[1,4,1,128]{3,1,2,0:T(4,128)S(1)}, f32[1,4,1,128]{3,1,2,0:T(4,128)S(1)}, u32[]{:S(2)}, u32[]{:S(2)}) collective-permute-start(f32[1,4,1,128]{3,1,2,0:T(4,128)S(1)} %get-tuple-element.274), channel_id=1, source_target_pairs={{0,2},{2,4},{4,6},{1,3},{3,5},{5,7},{8,10},{10,12},{12,14},{9,11},... | collective-permute-start | bytes 6152 | tf_op jit(solution)/shard_map/ppermute | solution.py:17
  108.4 3.4 %collective-permute-start.9 = (f32[1,4,1,128]{3,1,2,0:T(4,128)S(1)}, f32[1,4,1,128]{3,1,2,0:T(4,128)S(1)}, u32[]{:S(2)}, u32[]{:S(2)}) collective-permute-start(f32[1,4,1,128]{3,1,2,0:T(4,128)S(1)} %get-tuple-element.275), channel_id=1, source_target_pairs={{2,0},{4,2},{6,4},{3,1},{5,3},{7,5},{10,8},{12,10},{14,12},{11,9},... | collective-permute-start | bytes 6152 | tf_op jit(solution)/shard_map/ppermute | solution.py:20
  111.9 4.4 %collective-permute-start.11 = (f32[1,4,34,1]{3,1,2,0:T(4,128)S(1)}, f32[1,4,34,1]{3,1,2,0:T(4,128)S(1)}, u32[]{:S(2)}, u32[]{:S(2)}) collective-permute-start(f32[1,4,34,1]{3,1,2,0:T(4,128)S(1)} %get-tuple-element.269), channel_id=1, source_target_pairs={{1,0},{3,2},{5,4},{7,6},{9,8},{11,10},{13,12},{15,14},{17,16},{19,... | collective-permute-start | bytes 1640 | tf_op jit(solution)/shard_map/ppermute | solution.py:20
  113.4 6.2 %collective-permute-start.10 = (f32[1,4,34,1]{3,1,2,0:T(4,128)S(1)}, f32[1,4,34,1]{3,1,2,0:T(4,128)S(1)}, u32[]{:S(2)}, u32[]{:S(2)}) collective-permute-start(f32[1,4,34,1]{3,1,2,0:T(4,128)S(1)} %get-tuple-element.268), channel_id=1, source_target_pairs={{0,1},{2,3},{4,5},{6,7},{8,9},{10,11},{12,13},{14,15},{16,17},{18,... | collective-permute-start | bytes 1640 | tf_op jit(solution)/shard_map/ppermute | solution.py:17
  128.8 68.9 %collective-permute-start.13 = (f32[2,4,1,128]{3,1,2,0:T(4,128)S(1)}, f32[2,4,1,128]{3,1,2,0:T(4,128)S(1)}, u32[]{:S(2)}, u32[]{:S(2)}) collective-permute-start(f32[2,4,1,128]{3,1,2,0:T(4,128)S(1)} %get-tuple-element.261), channel_id=1, source_target_pairs={{2,0},{4,2},{6,4},{3,1},{5,3},{7,5},{10,8},{12,10},{14,12},{11,9},... | collective-permute-start | bytes 12296 | tf_op jit(solution)/shard_map/ppermute | solution.py:20
  130.1 67.6 %collective-permute-start.12 = (f32[2,4,1,128]{3,1,2,0:T(4,128)S(1)}, f32[2,4,1,128]{3,1,2,0:T(4,128)S(1)}, u32[]{:S(2)}, u32[]{:S(2)}) collective-permute-start(f32[2,4,1,128]{3,1,2,0:T(4,128)S(1)} %get-tuple-element.260), channel_id=1, source_target_pairs={{0,2},{2,4},{4,6},{1,3},{3,5},{5,7},{8,10},{10,12},{12,14},{9,11},... | collective-permute-start | bytes 12296 | tf_op jit(solution)/shard_map/ppermute | solution.py:17
  165.9 65.6 %collective-permute-start.20 = (f32[1,32,128]{2,1,0:T(8,128)S(1)}, f32[1,32,128]{2,1,0:T(8,128)S(1)}, u32[]{:S(2)}, u32[]{:S(2)}) collective-permute-start(f32[1,32,128]{2,1,0:T(8,128)S(1)} %bitcast.165), channel_id=1, source_target_pairs={{0,24},{8,0},{16,8},{24,16},{1,25},{9,1},{17,9},{25,17},{2,26},{10... | collective-permute-start | bytes 49160 | tf_op jit(solution)/shard_map/ppermute | solution.py:175
  197.9 6.3 %collective-permute-start.15 = (f32[2,4,34,1]{3,1,2,0:T(4,128)S(1)}, f32[2,4,34,1]{3,1,2,0:T(4,128)S(1)}, u32[]{:S(2)}, u32[]{:S(2)}) collective-permute-start(f32[2,4,34,1]{3,1,2,0:T(4,128)S(1)} %get-tuple-element.255), channel_id=1, source_target_pairs={{1,0},{3,2},{5,4},{7,6},{9,8},{11,10},{13,12},{15,14},{17,16},{19,... | collective-permute-start | bytes 3272 | tf_op jit(solution)/shard_map/ppermute | solution.py:20
  201.6 6.9 %collective-permute-start.14 = (f32[2,4,34,1]{3,1,2,0:T(4,128)S(1)}, f32[2,4,34,1]{3,1,2,0:T(4,128)S(1)}, u32[]{:S(2)}, u32[]{:S(2)}) collective-permute-start(f32[2,4,34,1]{3,1,2,0:T(4,128)S(1)} %get-tuple-element.254), channel_id=1, source_target_pairs={{0,1},{2,3},{4,5},{6,7},{8,9},{10,11},{12,13},{14,15},{16,17},{18,... | collective-permute-start | bytes 3272 | tf_op jit(solution)/shard_map/ppermute | solution.py:17
  231.6 4.8 %collective-permute-start.21 = (f32[2,32,128]{2,1,0:T(8,128)S(1)}, f32[2,32,128]{2,1,0:T(8,128)S(1)}, u32[]{:S(2)}, u32[]{:S(2)}) collective-permute-start(f32[2,32,128]{2,1,0:T(8,128)S(1)} %pad_maximum_fusion.9), channel_id=1, source_target_pairs={{0,16},{8,24},{16,0},{24,8},{1,17},{9,25},{17,1},{25,9},{2,18},{10... | collective-permute-start | bytes 98312 | tf_op jit(solution)/shard_map/ppermute | solution.py:175
  (5 other events, 147.2 us)
